TPU v7x, 256 devices: a whole 4x4x8 slice. The times are simulated.
256 devices in a mesh: row: 32 (over y, z), col: 8 (over x, core).
Axes of the slice: x: 4, y: 4, z: 8, core: 2. Of those that a mesh axis runs over, the one named last changes fastest.
Arguments:
- load_currents: float32 [16, 256, 128, 128], P(None, 'row', 'col'), may hold values from -24 to 24
- block_library: float32 [8, 128, 128], replicated, may hold values from -4.0625 to 24.1, as said below
- strap_conductance: float32 [2, 128], replicated, may hold values from 0.5 to 4
- block_types: int32 [256, 128], P('row', 'col'), may hold values from 0 to 7
- aggregate_map: int32 [256, 128], P('row', 'col'), may hold values from 0 to 255, as said below
Outputs:
- node_voltage: float32 [16, 256, 128, 128], P(None, 'row', 'col')
- residual: float32 [16, 256, 128, 128], P(None, 'row', 'col')
Inputs may be any that keep to these rules, and one draw needn't show every extreme that they name: `aggregate_map`: each aggregate id names an aggregate of one column group of 16 block columns; the same id in another column group is another aggregate. Every aggregate of every column group holds at least one block. `block_library`: each library block is symmetric positive definite, with nonpositive off-diagonal entries and positive row sums.
All inputs are finite; a program needn't handle non-finite values.
Results may differ from a plain program's by a relative error of at most 0.0003.
Values sent between devices are 32-bit elements; how exact they have to be, the bound alone decides.
A program may use at most 64 MiB of HBM per device.

v0:
```python
import jax
import jax.numpy as jnp
from jax import lax
from jax.sharding import PartitionSpec as P

SWEEPS = 3
ITERS = 2
AGR = 4
AGC = 4


def padded_2(array, sides, width):
    for axis, dim in sides:
        size, length = (lax.axis_size(axis), array.shape[dim])
        up = [(i, (i + 1) % size) for i in range(size - 1)]
        down = [(j, i) for i, j in up]
        last = lax.slice_in_dim(array, length - width, length, axis=dim)
        first = lax.slice_in_dim(array, 0, width, axis=dim)
        before = lax.ppermute(last, axis, up)
        after = lax.ppermute(first, axis, down)
        array = jnp.concatenate([before, array, after], axis=dim)
    return array


def from_behind(array, axis, by):
    length = lax.axis_size(axis)
    pairs = [(i, i + by) for i in range(length) if 0 <= i + by < length]
    return lax.ppermute(array, axis, pairs)


def coarse_terms(group_ids, group_types, block_sums, north_weight, east_weight, count):
    centre = block_sums[group_types] + 2.0 * north_weight + 2.0 * east_weight
    flat = group_ids.reshape(-1)
    upper = group_ids[:-1].reshape(-1)
    lower = group_ids[1:].reshape(-1)
    left = group_ids[:, :-1].reshape(-1)
    right = group_ids[:, 1:].reshape(-1)
    index = jnp.concatenate(
        [
            flat * count + flat,
            upper * count + lower,
            lower * count + upper,
            left * count + right,
            right * count + left,
        ]
    )
    values = jnp.concatenate(
        [
            centre.reshape(-1),
            -north_weight * jnp.ones((2 * upper.shape[0],), jnp.float32),
            -east_weight * jnp.ones((2 * left.shape[0],), jnp.float32),
        ]
    )
    return jax.ops.segment_sum(values, index, num_segments=count * count).reshape(count, count)


def alignment_sum(residual, zeta):
    return lax.psum(jnp.sum(residual * zeta, axis=(1, 2, 3)), ("row", "col"))


def on_device(load_currents, block_library, strap_conductance, block_types, aggregate_map):
    sizings, rows_local, cols_local, nodes = load_currents.shape
    blocks = rows_local * cols_local
    count = rows_local * lax.axis_size("row") // AGR * (cols_local // AGC)
    picked = block_library[block_types.reshape(-1)]
    couple = 2.0 * strap_conductance[0] + 2.0 * strap_conductance[1]
    diag_library = jnp.diagonal(block_library, axis1=1, axis2=2)
    diagonal = diag_library[block_types] + couple
    block_sums = jnp.sum(block_library, axis=(1, 2))
    north_weight = jnp.sum(strap_conductance[0])
    east_weight = jnp.sum(strap_conductance[1])

    def block_products(field):
        flat = field.reshape(sizings, blocks, nodes)
        product = jnp.einsum("bij,sbj->sbi", picked, flat, precision=lax.Precision.HIGHEST)
        return product.reshape(sizings, rows_local, cols_local, nodes)

    local_matrix = coarse_terms(
        aggregate_map, block_types, block_sums, north_weight, east_weight, count
    )
    below_ids = from_behind(aggregate_map[0], "row", -1)
    present = (lax.axis_index("row") < lax.axis_size("row") - 1).astype(jnp.float32)
    bottom_ids = aggregate_map[-1]
    cross_index = jnp.concatenate([bottom_ids * count + below_ids, below_ids * count + bottom_ids])
    cross_values = -north_weight * present * jnp.ones((2 * cols_local,), jnp.float32)
    cross_matrix = jax.ops.segment_sum(
        cross_values, cross_index, num_segments=count * count
    ).reshape(count, count)
    coarse_matrix = lax.psum(local_matrix + cross_matrix, "row")
    factor = jnp.linalg.cholesky(coarse_matrix)
    flat_ids = aggregate_map.reshape(-1)

    def smooth(residual):
        result = residual / diagonal
        for sweep in range(SWEEPS - 1):
            image = block_products(result) + couple * result
            result = result + (residual - image) / diagonal
        return result

    def coarse_part(residual):
        sums = residual.sum(-1).reshape(sizings, blocks).T
        local = jax.ops.segment_sum(sums, flat_ids, num_segments=count)
        gathered = lax.psum(local, "row")
        solved = jax.scipy.linalg.cho_solve((factor, True), gathered)
        return solved[flat_ids].T.reshape(sizings, rows_local, cols_local)[..., None]

    def precondition(residual):
        return smooth(residual) + coarse_part(residual)

    node_voltage = jnp.zeros_like(load_currents)
    residual = load_currents
    zeta = precondition(residual)
    direction = zeta
    aligned = alignment_sum(residual, zeta)
    for iteration in range(ITERS):
        padded = padded_2(direction, (("row", 1), ("col", 2)), 1)
        north = padded[:, :-2, 1:-1]
        south = padded[:, 2:, 1:-1]
        west = padded[:, 1:-1, :-2]
        east = padded[:, 1:-1, 2:]
        lateral = strap_conductance[0] * (2.0 * direction - north - south) + strap_conductance[
            1
        ] * (2.0 * direction - west - east)
        image = block_products(direction) + lateral
        curvature = lax.psum(jnp.sum(direction * image, axis=(1, 2, 3)), ("row", "col"))
        step_size = (aligned / curvature)[:, None, None, None]
        node_voltage = node_voltage + step_size * direction
        residual = residual - step_size * image
        if iteration + 1 < ITERS:
            zeta = precondition(residual)
            fresh = alignment_sum(residual, zeta)
            blend = (fresh / aligned)[:, None, None, None]
            direction = zeta + blend * direction
            aligned = fresh
    return (node_voltage, residual)


def solution(mesh):
    placed = (P(None, "row", "col", None), P(), P(), P("row", "col"), P("row", "col"))
    return jax.shard_map(
        on_device,
        mesh=mesh,
        in_specs=placed,
        out_specs=(P(None, "row", "col", None), P(None, "row", "col", None)),
        check_vma=False,
    )
```

profile of v0, /device:TPU:1, one launch (start us, length us, event | category | flops | bytes accessed | tf_op | source)
XLA Modules:
  0.0 772.2 jit_solution(3687097905419126397)
XLA Ops:
  8.0 1.3 collective-permute-start
  9.3 1.4 slice_reduce_fusion.1
  18.7 5.9 copy.47
  25.0 1.8 gather_fusion
  26.8 1.2 gather_fusion.3
  28.8 4.3 gather_fusion.2
  33.8 16.3 %fusion.50 = f32[128,16,128]{2,1,0:T(8,128)S(1)} fusion(f32[16,128,128]{2,0,1:T(8,128)S(1)} %bitcast.139, f32[128,128,128]{2,1,0:T(8,128)} %gather_fusion.2), kind=kOutput, calls=%fused_computation.144 | convolution fusion | flops 402653184 | bytes 10485760 | tf_op jit(solution)/shard_map/bij,sbj->sbi/dot_general | solution.py:75
  50.8 14.2 %fusion.51 = f32[128,16,128]{2,1,0:T(8,128)} fusion(f32[16,128,128]{2,0,1:T(8,128)S(1)} %bitcast.140, f32[128,128,128]{2,1,0:T(8,128)S(1)} %bitcast.127), kind=kOutput, calls=%fused_computation.145 | convolution fusion | flops 402653184 | bytes 10485760 | tf_op jit(solution)/shard_map/bij,sbj->sbi/dot_general | solution.py:75
  66.2 4.7 scatter_custom_fusion
  72.3 1.7 scatter_custom_fusion.1
  74.0 120.5 %psum.50 = f32[256,16]{0,1:T(8,128)S(1)} all-reduce(f32[256,16]{0,1:T(8,128)S(1)} %copy.55), channel_id=1, replica_groups=mesh['row'=32,'col'=8] {'row'}, use_global_device_ids=true, to_apply=%region_11.12 | all-reduce | flops 4096 | bytes 32768 | tf_op jit(solution)/shard_map/psum | solution.py:103
  194.5 23.7 %all-reduce.5.cloned.1.call-done = f32[256,256]{0,1:T(8,128)} async-done(((f32[256,256]{0,1:T(8,128)}), f32[256,256]{0,1:T(8,128)}) %all-reduce.5.cloned.1.call-update) | async-done | bytes 262160 | tf_op jit(solution)/shard_map/psum | solution.py:89
  218.2 1.1 copy.53
  220.3 11.7 %cholesky.50 = f32[128,128]{1,0:T(8,128)S(1)} custom-call(f32[128,128]{1,0:T(8,128)S(1)} %cholesky.118), custom_call_target="Cholesky" | custom-call | tf_op jit(solution)/shard_map/jit(cholesky)/cholesky | solution.py:90
  232.1 9.8 %custom-call.16 = f32[1,128,128]{1,2,0:T(8,128)S(1)} custom-call(f32[1,128,128]{2,1,0:T(8,128)S(1)} %get-tuple-element.55), custom_call_target="InvertDiagBlocksLowerTriangular" | custom-call | tf_op jit(solution)/shard_map/jit(cholesky)/cholesky | solution.py:90
  242.4 11.7 %cholesky.105 = f32[128,128]{1,0:T(8,128)S(1)} custom-call(f32[128,128]{1,0:T(8,128)S(1)} %convolution_subtract_fusion), custom_call_target="Cholesky" | custom-call | tf_op jit(solution)/shard_map/jit(cholesky)/cholesky | solution.py:90
  256.1 3.8 while.4
  256.7 1.3 bitcast_dynamic-update-slice_fusion.2
  258.6 1.3 bitcast_dynamic-update-slice_fusion.2
  260.0 19.8 %custom-call.20 = f32[2,128,128]{1,2,0:T(8,128)S(1)} custom-call(f32[2,128,128]{2,1,0:T(8,128)S(1)} %get-tuple-element.17), custom_call_target="InvertDiagBlocksLowerTriangular" | custom-call | tf_op jit(solution)/shard_map/jit(_cho_solve)/triangular_solve | solution.py:104
  281.8 2.0 add_add_fusion.1
  283.8 1.9 collective-permute-start.1
  285.7 1.3 collective-permute-start.2
  287.6 4.0 collective-permute-done.2
  291.6 9.7 %collective-permute-start.3 = (f32[16,10,1,128]{3,0,2,1:T(8,128)S(1)}, f32[16,10,1,128]{3,0,2,1:T(8,128)S(1)}, u32[]{:S(2)}, u32[]{:S(2)}) collective-permute-start(f32[16,10,1,128]{3,0,2,1:T(8,128)S(1)} %get-tuple-element.44), channel_id=1, source_target_pairs={{0,1},{1,2},{2,3},{3,4},{4,5},{5,6},{6,7},{8,9},{9,10},{10,11},{11... | collective-permute-start | bytes 245768 | tf_op jit(solution)/shard_map/ppermute | solution.py:19
  301.4 1.9 collective-permute-start.4
  303.3 15.4 %fusion.52 = f32[128,16,128]{2,1,0:T(8,128)S(1)} fusion(f32[16,128,128]{2,0,1:T(8,128)S(1)} %bitcast.130, f32[128,128,128]{2,1,0:T(8,128)} %gather_fusion.2), kind=kOutput, calls=%fused_computation.146 | convolution fusion | flops 402653184 | bytes 10485760 | tf_op jit(solution)/shard_map/bij,sbj->sbi/dot_general | solution.py:75
  318.7 1.8 multiply_reduce_fusion.2
  320.5 77.0 %all-reduce.2 = (f32[16]{0:T(128)S(1)}, f32[16]{0:T(128)S(1)}) all-reduce(f32[16]{0:T(128)S(1)} %get-tuple-element.22, f32[16]{0:T(128)S(1)} %get-tuple-element.21), channel_id=1, replica_groups=mesh['row'=32,'col'=8] {'row','col'}, use_global_device_ids=true, to_apply=%region_13.15 | all-reduce | flops 32 | bytes 256 | tf_op jit(solution)/shard_map/psum | solution.py:58
  397.6 2.1 broadcast_divide_fusion
  399.7 15.8 %divide_add_fusion = (f32[16,8,16,128]{3,0,2,1:T(8,128)S(1)}, f32[16,8,16]{0,2,1:T(8,128)S(1)}, f32[128,16,128]{2,1,0:T(8,128)S(1)}) fusion(f32[16,8,16,128]{3,0,2,1:T(8,128)S(1)} %get-tuple-element.38, f32[128]{0:T(128)S(1)} %add_multiply_fusion, f32[8,16,128]{2,1,0:T(8,128)S(1)} %broadcast_add_fusion, f32[16,128,128]{2,0,1:T(8,128)S(1)} %bitcast.137, ...), kind=kOutput, calls=%fused_computation.54 | convolution fusion | flops 404486144 | bytes 12657152 | tf_op jit(solution)/shard_map/bij,sbj->sbi/dot_general | solution.py:75
  415.5 14.0 %fusion.53 = f32[128,16,128]{2,1,0:T(8,128)} fusion(f32[16,128,128]{2,0,1:T(8,128)S(1)} %bitcast.138, f32[128,128,128]{2,1,0:T(8,128)S(1)} %bitcast.129), kind=kOutput, calls=%fused_computation.147 | convolution fusion | flops 402653184 | bytes 10485760 | tf_op jit(solution)/shard_map/bij,sbj->sbi/dot_general | solution.py:75
  429.6 1.9 scatter_custom_fusion.2
  432.4 110.3 %psum.53 = f32[256,16]{0,1:T(8,128)S(1)} all-reduce(f32[256,16]{0,1:T(8,128)S(1)} %copy.61), channel_id=1, replica_groups=mesh['row'=32,'col'=8] {'row'}, use_global_device_ids=true, to_apply=%region_18.20 | all-reduce | flops 4096 | bytes 32768 | tf_op jit(solution)/shard_map/psum | solution.py:103
  548.0 1.9 multiply_reduce_fusion.1
  549.9 100.2 %psum.54 = f32[16]{0:T(128)S(1)} all-reduce(f32[16]{0:T(128)S(1)} %multiply_reduce_fusion.1), channel_id=1, replica_groups=mesh['row'=32,'col'=8] {'row','col'}, use_global_device_ids=true, to_apply=%region_20.22 | all-reduce | flops 16 | bytes 128 | tf_op jit(solution)/shard_map/psum | solution.py:58
  650.7 2.1 multiply_add_fusion.1
  652.8 3.7 collective-permute-start.5
  656.5 1.3 collective-permute-start.6
  658.7 3.6 collective-permute-done.6
  662.3 4.3 collective-permute-start.7
  666.5 1.9 collective-permute-start.8
  668.5 15.4 %fusion.54 = f32[128,16,128]{2,1,0:T(8,128)S(1)} fusion(f32[16,128,128]{2,0,1:T(8,128)S(1)} %bitcast.131, f32[128,128,128]{2,1,0:T(8,128)} %gather_fusion.2), kind=kOutput, calls=%fused_computation.148 | convolution fusion | flops 402653184 | bytes 10485760 | tf_op jit(solution)/shard_map/bij,sbj->sbi/dot_general | solution.py:75
  683.9 1.5 multiply_reduce_fusion
  685.3 75.4 %psum.55 = f32[16]{0:T(128)S(1)} all-reduce(f32[16]{0:T(128)S(1)} %get-tuple-element.35), channel_id=1, replica_groups=mesh['row'=32,'col'=8] {'row','col'}, use_global_device_ids=true, to_apply=%region_22.24 | all-reduce | flops 16 | bytes 128 | tf_op jit(solution)/shard_map/psum | solution.py:125
  760.8 1.6 multiply_subtract_fusion
  762.3 1.3 copy.63
  763.6 1.3 copy.64
  (119 shorter events, 25.1 us)
Async XLA Ops:
  7.2 17.4 %copy-start = (f32[8,128,128]{2,1,0:T(8,128)S(1)}, f32[8,128,128]{2,1,0:T(8,128)}, u32[]{:S(2)}) copy-start(f32[8,128,128]{2,1,0:T(8,128)} %param.8) | copy-start | bytes 1572868
  7.2 211.1 %all-reduce.5.cloned.1.call-start = ((), (), s32[]{:S(2)}) async-start(), calls=%async_computation | async-start | bytes 524288 | tf_op jit(solution)/shard_map/psum | solution.py:89
  8.0 57.3 %collective-permute-start = (s32[16]{0:T(128)S(1)}, s32[16]{0:T(128)S(1)}, u32[]{:S(2)}, u32[]{:S(2)}) collective-permute-start(s32[16]{0:T(128)S(1)} %slice_bitcast_fusion.10), channel_id=1, source_target_pairs={{8,0},{16,8},{24,16},{32,24},{40,32},{48,40},{56,48},{64,56},{72,6... | collective-permute-start | bytes 200 | tf_op jit(solution)/shard_map/ppermute | solution.py:28
  15.6 56.7 %copy-start.6 = (s32[128]{0:T(128)}, s32[128]{0:T(128)S(1)}, u32[]{:S(2)}) copy-start(s32[128]{0:T(128)S(1)} %reshape.186) | copy-start | bytes 1540
  28.8 4.3 copy-start.1
  33.1 17.7 %slice-start = ((s8[8388608]{0:T(1024)(128)(4,1)}), s8[4194304]{0:T(1024)(128)(4,1)S(1)}, s32[]{:S(2)}) async-start(s8[8388608]{0:T(1024)(128)(4,1)} %bitcast.126), calls=%async_computation.1 | async-start | bytes 8388608
  33.8 17.1 %slice-start.1 = ((s8[8388608]{0:T(1024)(128)(4,1)}), s8[4194304]{0:T(1024)(128)(4,1)S(1)}, s32[]{:S(2)}) async-start(s8[8388608]{0:T(1024)(128)(4,1)} %bitcast.126), calls=%async_computation.2 | async-start | bytes 8388608
  279.8 1.2 copy-start.3
  283.8 3.8 collective-permute-start.1
  285.7 5.9 collective-permute-start.2
  291.6 27.0 %collective-permute-start.3 = (f32[16,10,1,128]{3,0,2,1:T(8,128)S(1)}, f32[16,10,1,128]{3,0,2,1:T(8,128)S(1)}, u32[]{:S(2)}, u32[]{:S(2)}) collective-permute-start(f32[16,10,1,128]{3,0,2,1:T(8,128)S(1)} %get-tuple-element.44), channel_id=1, source_target_pairs={{0,1},{1,2},{2,3},{3,4},{4,5},{5,6},{6,7},{8,9},{9,10},{10,11},{11... | collective-permute-start | bytes 245768 | tf_op jit(solution)/shard_map/ppermute | solution.py:19
  301.4 17.3 %collective-permute-start.4 = (f32[16,10,1,128]{3,0,2,1:T(8,128)S(1)}, f32[16,10,1,128]{3,0,2,1:T(8,128)S(1)}, u32[]{:S(2)}, u32[]{:S(2)}) collective-permute-start(f32[16,10,1,128]{3,0,2,1:T(8,128)S(1)} %get-tuple-element.45), channel_id=1, source_target_pairs={{1,0},{2,1},{3,2},{4,3},{5,4},{6,5},{7,6},{9,8},{10,9},{11,10},{12... | collective-permute-start | bytes 245768 | tf_op jit(solution)/shard_map/ppermute | solution.py:20
  397.6 2.1 copy-start.7
  397.6 2.1 copy-start.4
  397.6 17.9 %slice-start.2 = ((s8[8388608]{0:T(1024)(128)(4,1)}), s8[4194304]{0:T(1024)(128)(4,1)S(1)}, s32[]{:S(2)}) async-start(s8[8388608]{0:T(1024)(128)(4,1)} %bitcast.128), calls=%async_computation.3 | async-start | bytes 8388608
  399.7 15.8 %slice-start.3 = ((s8[8388608]{0:T(1024)(128)(4,1)}), s8[4194304]{0:T(1024)(128)(4,1)S(1)}, s32[]{:S(2)}) async-start(s8[8388608]{0:T(1024)(128)(4,1)} %bitcast.128), calls=%async_computation.4 | async-start | bytes 8388608
  415.5 234.6 %copy-start.2 = (f32[128,16,128]{2,1,0:T(8,128)}, f32[128,16,128]{2,1,0:T(8,128)S(1)}, u32[]{:S(2)}) copy-start(f32[128,16,128]{2,1,0:T(8,128)S(1)} %get-tuple-element.72) | copy-start | bytes 3145732
  652.8 108.0 %copy-start.5 = (f32[16]{0:T(128)S(1)}, f32[16]{0:T(128)}, u32[]{:S(2)}) copy-start(f32[16]{0:T(128)} %copy-done.4) | copy-start | bytes 196
  652.8 5.8 collective-permute-start.5
  656.5 5.7 collective-permute-start.6
  662.3 21.6 %collective-permute-start.7 = (f32[16,10,1,128]{3,0,2,1:T(8,128)S(1)}, f32[16,10,1,128]{3,0,2,1:T(8,128)S(1)}, u32[]{:S(2)}, u32[]{:S(2)}) collective-permute-start(f32[16,10,1,128]{3,0,2,1:T(8,128)S(1)} %get-tuple-element.42), channel_id=1, source_target_pairs={{0,1},{1,2},{2,3},{3,4},{4,5},{5,6},{6,7},{8,9},{9,10},{10,11},{11... | collective-permute-start | bytes 245768 | tf_op jit(solution)/shard_map/ppermute | solution.py:19
  666.5 17.3 %collective-permute-start.8 = (f32[16,10,1,128]{3,0,2,1:T(8,128)S(1)}, f32[16,10,1,128]{3,0,2,1:T(8,128)S(1)}, u32[]{:S(2)}, u32[]{:S(2)}) collective-permute-start(f32[16,10,1,128]{3,0,2,1:T(8,128)S(1)} %get-tuple-element.43), channel_id=1, source_target_pairs={{1,0},{2,1},{3,2},{4,3},{5,4},{6,5},{7,6},{9,8},{10,9},{11,10},{12... | collective-permute-start | bytes 245768 | tf_op jit(solution)/shard_map/ppermute | solution.py:20
Sparse Core Ops, SparseCore 0:
  72.0 146.2 all-reduce.4
where the time goes:
time: 779 us; the launch traced here: 772 us
  blocking collectives  483 us (62%)
  matrix products  97.2 us (12%)
  other arithmetic  82.4 us (11%)
  waiting for transfers between devices  32.8 us (4%)
  local copies, waits for them, and re-layouts  30.2 us (4%)
  starting transfers between devices  27.3 us (4%)
  between operations  18.8 us (2%)
    psum x2, blocking collectives, coarse_part(): gathered = lax.psum(local, 'row')  231 us
    psum x2, blocking collectives, alignment_sum(): return lax.psum(jnp.sum(residual * zeta, axis=(1, 2, 3)), ('row', 'col'))  177 us
    dot_general x6, matrix products, block_products(): jnp.einsum('bij,sbj->sbi', picked, flat, precision=lax.Precision.HIGHEST)  91.1 us
    psum x1, blocking collectives, on_device(): lax.psum(jnp.sum(direction * image, axis=(1, 2, 3)), ('row', 'col'))  75.4 us
    another operation x6, other arithmetic, on_device(): factor = jnp.linalg.cholesky(coarse_matrix)  33.9 us
    psum x1, waiting for transfers between devices, on_device(): coarse_matrix = lax.psum(local_matrix + cross_matrix, 'row')  23.7 us
    another operation x6, other arithmetic, coarse_part(): solved = jax.scipy.linalg.cho_solve((factor, True), gathered)  19.9 us
    ppermute x4, starting transfers between devices, padded_2(): before = lax.ppermute(last, axis, up)  19.5 us
  transfers between devices with their start and end apart: 10, of which 5 were waited for; matrix products, arithmetic and copies ran while one was open for 11% of the time, Pallas kernels for 0%

commit v1 on v0

--- a/solution.py
+++ b/solution.py
@@ -100,7 +100,7 @@
     def coarse_part(residual):
         sums = residual.sum(-1).reshape(sizings, blocks).T
         local = jax.ops.segment_sum(sums, flat_ids, num_segments=count)
-        gathered = lax.psum(local, "row")
+        gathered = jnp.sum(lax.all_gather(local, "row"), axis=0)
         solved = jax.scipy.linalg.cho_solve((factor, True), gathered)
         return solved[flat_ids].T.reshape(sizings, rows_local, cols_local)[..., None]
 

time: 779 us -> 708 us (0.909)
  blocking collectives: 483 us -> 342 us
  waiting for transfers between devices: 32.8 us -> 95.5 us
    psum x2 -> x0, blocking collectives: 231 us -> none  [coarse_part(): gathered = lax.psum(local, 'row')]
    all_gather x0 -> x2, blocking collectives: none -> 105 us  [coarse_part(): gathered = jnp.sum(lax.all_gather(local, 'row'), axis=0)]
    psum x1, waiting for transfers between devices: 23.7 us -> 86.4 us  [on_device(): coarse_matrix = lax.psum(local_matrix + cross_matrix, 'row')]
    psum x2, blocking collectives: 177 us -> 161 us  [alignment_sum(): return lax.psum(jnp.sum(residual * zeta, axis=(1, 2, 3)), ('row', 'col'))]
  transfers between devices with their start and end apart: 10 -> 10, of which waited for: 5 -> 5; matrix products, arithmetic and copies ran while one was open for 11% -> 13% of each run, Pallas kernels for 0% -> 0%
where the time goes in v1:
time: 708 us; the launch traced here: 701 us
  blocking collectives  342 us (48%)
  matrix products  101 us (14%)
  waiting for transfers between devices  95.5 us (13%)
  other arithmetic  87.3 us (12%)
  local copies, waits for them, and re-layouts  29.6 us (4%)
  starting transfers between devices  26.3 us (4%)
  between operations  18.9 us (3%)
    psum x2, blocking collectives, alignment_sum(): return lax.psum(jnp.sum(residual * zeta, axis=(1, 2, 3)), ('row', 'col'))  161 us
    all_gather x2, blocking collectives, coarse_part(): gathered = jnp.sum(lax.all_gather(local, 'row'), axis=0)  105 us
    dot_general x6, matrix products, block_products(): jnp.einsum('bij,sbj->sbi', picked, flat, precision=lax.Precision.HIGHEST)  94.4 us
    psum x1, waiting for transfers between devices, on_device(): coarse_matrix = lax.psum(local_matrix + cross_matrix, 'row')  86.4 us
    psum x1, blocking collectives, on_device(): lax.psum(jnp.sum(direction * image, axis=(1, 2, 3)), ('row', 'col'))  76.1 us
    another operation x6, other arithmetic, on_device(): factor = jnp.linalg.cholesky(coarse_matrix)  34 us
    another operation x6, other arithmetic, coarse_part(): solved = jax.scipy.linalg.cho_solve((factor, True), gathered)  19.8 us
    ppermute x4, starting transfers between devices, padded_2(): before = lax.ppermute(last, axis, up)  18.6 us
  transfers between devices with their start and end apart: 10, of which 5 were waited for; matrix products, arithmetic and copies ran while one was open for 13% of the time, Pallas kernels for 0%

profile of v1, /device:TPU:1, one launch (start us, length us, event | category | flops | bytes accessed | tf_op | source)
XLA Modules:
  0.0 700.9 jit_solution(17341688851037991283)
XLA Ops:
  8.0 1.3 collective-permute-start
  11.6 1.4 slice_reduce_fusion.1
  18.7 5.8 copy.63
  25.6 4.3 gather_fusion.2
  29.9 1.8 gather_fusion
  31.8 1.2 gather_fusion.3
  34.4 16.3 %fusion.50 = f32[128,16,128]{2,1,0:T(8,128)S(1)} fusion(f32[16,128,128]{2,0,1:T(8,128)S(1)} %bitcast.141, f32[128,128,128]{2,1,0:T(8,128)} %gather_fusion.2), kind=kOutput, calls=%fused_computation.144 | convolution fusion | flops 402653184 | bytes 10485760 | tf_op jit(solution)/shard_map/bij,sbj->sbi/dot_general | solution.py:75
  51.4 14.2 %fusion.51 = f32[128,16,128]{2,1,0:T(8,128)} fusion(f32[16,128,128]{2,0,1:T(8,128)S(1)} %bitcast.142, f32[128,128,128]{2,1,0:T(8,128)S(1)} %bitcast.129), kind=kOutput, calls=%fused_computation.145 | convolution fusion | flops 402653184 | bytes 10485760 | tf_op jit(solution)/shard_map/bij,sbj->sbi/dot_general | solution.py:75
  67.8 4.7 scatter_custom_fusion
  73.5 57.6 %all-gather = f32[8192,16]{1,0:T(8,128)} all-gather(f32[256,16]{1,0:T(8,128)S(1)} %scatter_custom_fusion.1), channel_id=2, replica_groups=mesh['row'=32,'col'=8] {'row'}, dimensions={0}, use_global_device_ids=true | all-gather | bytes 540672 | tf_op jit(solution)/shard_map/all_gather | solution.py:103
  131.1 2.5 reduce_sum.103
  133.7 86.4 %all-reduce.5.cloned.1.call-done = f32[256,256]{0,1:T(8,128)} async-done(((f32[256,256]{0,1:T(8,128)}), f32[256,256]{0,1:T(8,128)}) %all-reduce.5.cloned.1.call-update) | async-done | bytes 262160 | tf_op jit(solution)/shard_map/psum | solution.py:89
  222.2 11.7 %cholesky.50 = f32[128,128]{1,0:T(8,128)S(1)} custom-call(f32[128,128]{1,0:T(8,128)S(1)} %cholesky.118), custom_call_target="Cholesky" | custom-call | tf_op jit(solution)/shard_map/jit(cholesky)/cholesky | solution.py:90
  234.0 9.8 %custom-call.16 = f32[1,128,128]{1,2,0:T(8,128)S(1)} custom-call(f32[1,128,128]{2,1,0:T(8,128)S(1)} %get-tuple-element.57), custom_call_target="InvertDiagBlocksLowerTriangular" | custom-call | tf_op jit(solution)/shard_map/jit(cholesky)/cholesky | solution.py:90
  244.3 11.7 %cholesky.105 = f32[128,128]{1,0:T(8,128)S(1)} custom-call(f32[128,128]{1,0:T(8,128)S(1)} %convolution_subtract_fusion), custom_call_target="Cholesky" | custom-call | tf_op jit(solution)/shard_map/jit(cholesky)/cholesky | solution.py:90
  258.1 4.1 while.4
  258.9 1.4 bitcast_dynamic-update-slice_fusion.2
  260.9 1.4 bitcast_dynamic-update-slice_fusion.2
  262.2 19.7 %custom-call.20 = f32[2,128,128]{1,2,0:T(8,128)S(1)} custom-call(f32[2,128,128]{2,1,0:T(8,128)S(1)} %get-tuple-element.17), custom_call_target="InvertDiagBlocksLowerTriangular" | custom-call | tf_op jit(solution)/shard_map/jit(_cho_solve)/triangular_solve | solution.py:104
  284.0 2.0 add_add_fusion.1
  286.0 1.8 collective-permute-start.1
  287.8 1.3 collective-permute-start.2
  289.8 4.0 collective-permute-done.2
  293.8 9.8 %collective-permute-start.3 = (f32[16,10,1,128]{3,0,2,1:T(8,128)S(1)}, f32[16,10,1,128]{3,0,2,1:T(8,128)S(1)}, u32[]{:S(2)}, u32[]{:S(2)}) collective-permute-start(f32[16,10,1,128]{3,0,2,1:T(8,128)S(1)} %get-tuple-element.46), channel_id=1, source_target_pairs={{0,1},{1,2},{2,3},{3,4},{4,5},{5,6},{6,7},{8,9},{9,10},{10,11},{11... | collective-permute-start | bytes 245768 | tf_op jit(solution)/shard_map/ppermute | solution.py:19
  303.6 1.9 collective-permute-start.4
  305.5 15.4 %fusion.52 = f32[128,16,128]{2,1,0:T(8,128)S(1)} fusion(f32[16,128,128]{2,0,1:T(8,128)S(1)} %bitcast.130, f32[128,128,128]{2,1,0:T(8,128)} %gather_fusion.2), kind=kOutput, calls=%fused_computation.146 | convolution fusion | flops 402653184 | bytes 10485760 | tf_op jit(solution)/shard_map/bij,sbj->sbi/dot_general | solution.py:75
  320.9 1.8 multiply_reduce_fusion.2
  322.7 77.3 %all-reduce.2 = (f32[16]{0:T(128)S(1)}, f32[16]{0:T(128)S(1)}) all-reduce(f32[16]{0:T(128)S(1)} %get-tuple-element.24, f32[16]{0:T(128)S(1)} %get-tuple-element.23), channel_id=1, replica_groups=mesh['row'=32,'col'=8] {'row','col'}, use_global_device_ids=true, to_apply=%region_13.15 | all-reduce | flops 32 | bytes 256 | tf_op jit(solution)/shard_map/psum | solution.py:58
  400.0 1.9 broadcast_divide_fusion
  402.0 16.2 %divide_add_fusion = (f32[16,8,16,128]{3,0,2,1:T(8,128)}, f32[16,8,16]{0,2,1:T(8,128)S(1)}, f32[128,16,128]{2,1,0:T(8,128)S(1)}) fusion(f32[16,8,16,128]{3,0,2,1:T(8,128)S(1)} %get-tuple-element.40, f32[128]{0:T(128)S(1)} %add_multiply_fusion, f32[8,16,128]{2,1,0:T(8,128)S(1)} %broadcast_add_fusion, f32[16,128,128]{2,0,1:T(8,128)S(1)} %bitcast.140, ...), kind=kOutput, calls=%fused_computation.54 | convolution fusion | flops 404486144 | bytes 12657152 | tf_op jit(solution)/shard_map/bij,sbj->sbi/dot_general | solution.py:75
  418.2 1.8 scatter_custom_fusion.2
  420.0 47.3 %all-gather.1 = f32[8192,16]{1,0:T(8,128)} all-gather(f32[256,16]{1,0:T(8,128)} %scatter_custom_fusion.2), channel_id=3, replica_groups=mesh['row'=32,'col'=8] {'row'}, dimensions={0}, use_global_device_ids=true | all-gather | bytes 540672 | tf_op jit(solution)/shard_map/all_gather | solution.py:103
  467.2 3.1 reduce_sum.107
  471.5 16.6 %fusion.53 = f32[128,16,128]{2,1,0:T(8,128)} fusion(f32[16,128,128]{2,0,1:T(8,128)} %bitcast.139, f32[128,128,128]{2,1,0:T(8,128)} %gather_fusion.2), kind=kOutput, calls=%fused_computation.147 | convolution fusion | flops 402653184 | bytes 10485760 | tf_op jit(solution)/shard_map/bij,sbj->sbi/dot_general | solution.py:75
  492.6 1.9 multiply_reduce_fusion.1
  494.5 84.1 %psum.38 = f32[16]{0:T(128)S(1)} all-reduce(f32[16]{0:T(128)S(1)} %multiply_reduce_fusion.1), channel_id=1, replica_groups=mesh['row'=32,'col'=8] {'row','col'}, use_global_device_ids=true, to_apply=%region_20.22 | all-reduce | flops 16 | bytes 128 | tf_op jit(solution)/shard_map/psum | solution.py:58
  579.3 2.1 multiply_add_fusion.1
  581.4 3.3 collective-permute-start.5
  584.8 1.3 collective-permute-start.6
  586.9 3.6 collective-permute-done.6
  590.5 3.7 collective-permute-start.7
  594.2 1.9 collective-permute-start.8
  596.1 15.7 %fusion.54 = f32[128,16,128]{2,1,0:T(8,128)S(1)} fusion(f32[16,128,128]{2,0,1:T(8,128)S(1)} %bitcast.131, f32[128,128,128]{2,1,0:T(8,128)} %gather_fusion.2), kind=kOutput, calls=%fused_computation.148 | convolution fusion | flops 402653184 | bytes 10485760 | tf_op jit(solution)/shard_map/bij,sbj->sbi/dot_general | solution.py:75
  611.8 1.5 multiply_reduce_fusion
  613.3 76.1 %psum.39 = f32[16]{0:T(128)S(1)} all-reduce(f32[16]{0:T(128)S(1)} %get-tuple-element.37), channel_id=1, replica_groups=mesh['row'=32,'col'=8] {'row','col'}, use_global_device_ids=true, to_apply=%region_22.24 | all-reduce | flops 16 | bytes 128 | tf_op jit(solution)/shard_map/psum | solution.py:125
  689.4 1.6 multiply_subtract_fusion
  690.9 1.3 copy.80
  692.2 1.3 copy.79
  (129 shorter events, 27.0 us)
Async XLA Ops:
  7.2 17.3 %copy-start = (f32[8,128,128]{2,1,0:T(8,128)S(1)}, f32[8,128,128]{2,1,0:T(8,128)}, u32[]{:S(2)}) copy-start(f32[8,128,128]{2,1,0:T(8,128)} %param.8) | copy-start | bytes 1572868
  7.2 18.0 %copy-start.1 = (f32[16,8,16,128]{3,2,1,0:T(8,128)S(1)}, f32[16,8,16,128]{3,2,1,0:T(8,128)}, u32[]{:S(2)}) copy-start(f32[16,8,16,128]{3,2,1,0:T(8,128)} %param.7) | copy-start | bytes 3145732
  7.2 212.9 %all-reduce.5.cloned.1.call-start = ((), (), s32[]{:S(2)}) async-start(), calls=%async_computation | async-start | bytes 524288 | tf_op jit(solution)/shard_map/psum | solution.py:89
  8.0 58.9 %collective-permute-start = (s32[16]{0:T(128)S(1)}, s32[16]{0:T(128)S(1)}, u32[]{:S(2)}, u32[]{:S(2)}) collective-permute-start(s32[16]{0:T(128)S(1)} %slice_bitcast_fusion.10), channel_id=1, source_target_pairs={{8,0},{16,8},{24,16},{32,24},{40,32},{48,40},{56,48},{64,56},{72,6... | collective-permute-start | bytes 200 | tf_op jit(solution)/shard_map/ppermute | solution.py:28
  11.6 390.3 %copy-start.4 = (f32[128]{0:T(128)}, f32[128]{0:T(128)S(1)}, u32[]{:S(2)}) copy-start(f32[128]{0:T(128)S(1)} %add_multiply_fusion) | copy-start | bytes 1540
  13.0 307.9 %copy-start.6 = (f32[128]{0:T(128)}, f32[128]{0:T(128)S(1)}, u32[]{:S(2)}) copy-start(f32[128]{0:T(128)S(1)} %get-tuple-element.64) | copy-start | bytes 1540
  13.0 307.9 %copy-start.8 = (f32[128]{0:T(128)}, f32[128]{0:T(128)S(1)}, u32[]{:S(2)}) copy-start(f32[128]{0:T(128)S(1)} %get-tuple-element.65) | copy-start | bytes 1540
  33.7 17.7 %slice-start = ((s8[8388608]{0:T(1024)(128)(4,1)}), s8[4194304]{0:T(1024)(128)(4,1)S(1)}, s32[]{:S(2)}) async-start(s8[8388608]{0:T(1024)(128)(4,1)} %bitcast.128), calls=%async_computation.1 | async-start | bytes 8388608
  34.3 17.1 %slice-start.1 = ((s8[8388608]{0:T(1024)(128)(4,1)}), s8[4194304]{0:T(1024)(128)(4,1)S(1)}, s32[]{:S(2)}) async-start(s8[8388608]{0:T(1024)(128)(4,1)} %bitcast.128), calls=%async_computation.2 | async-start | bytes 8388608
  133.7 150.2 %copy-start.5 = (s32[1024]{0:T(1024)}, s32[1024]{0:T(1024)S(1)}, u32[]{:S(2)}) copy-start(s32[1024]{0:T(1024)S(1)} %pad_clamp_fusion) | copy-start | bytes 12292
  281.9 1.2 copy-start.3
  286.0 3.7 collective-permute-start.1
  287.8 5.9 collective-permute-start.2
  293.8 27.1 %collective-permute-start.3 = (f32[16,10,1,128]{3,0,2,1:T(8,128)S(1)}, f32[16,10,1,128]{3,0,2,1:T(8,128)S(1)}, u32[]{:S(2)}, u32[]{:S(2)}) collective-permute-start(f32[16,10,1,128]{3,0,2,1:T(8,128)S(1)} %get-tuple-element.46), channel_id=1, source_target_pairs={{0,1},{1,2},{2,3},{3,4},{4,5},{5,6},{6,7},{8,9},{9,10},{10,11},{11... | collective-permute-start | bytes 245768 | tf_op jit(solution)/shard_map/ppermute | solution.py:19
  303.6 17.3 %collective-permute-start.4 = (f32[16,10,1,128]{3,0,2,1:T(8,128)S(1)}, f32[16,10,1,128]{3,0,2,1:T(8,128)S(1)}, u32[]{:S(2)}, u32[]{:S(2)}) collective-permute-start(f32[16,10,1,128]{3,0,2,1:T(8,128)S(1)} %get-tuple-element.47), channel_id=1, source_target_pairs={{1,0},{2,1},{3,2},{4,3},{5,4},{6,5},{7,6},{9,8},{10,9},{11,10},{12... | collective-permute-start | bytes 245768 | tf_op jit(solution)/shard_map/ppermute | solution.py:20
  400.0 18.2 %copy-start.12 = (f32[16]{0:T(128)}, f32[16]{0:T(128)S(1)}, u32[]{:S(2)}) copy-start(f32[16]{0:T(128)S(1)} %get-tuple-element.35) | copy-start | bytes 196
  400.0 1.9 copy-start.10
  418.2 74.5 %copy-start.2 = (f32[128,16,128]{2,1,0:T(8,128)}, f32[128,16,128]{2,1,0:T(8,128)S(1)}, u32[]{:S(2)}) copy-start(f32[128,16,128]{2,1,0:T(8,128)S(1)} %get-tuple-element.74) | copy-start | bytes 3145732
  470.4 17.8 %slice-start.2 = ((f32[256,16]{1,0:T(8,128)}), f32[128,16]{1,0:T(8,128)S(1)}, s32[]{:S(2)}) async-start(f32[256,16]{1,0:T(8,128)} %reduce_sum.107), calls=%async_computation.3 | async-start | bytes 131072 | tf_op jit(solution)/shard_map/jit(_cho_solve)/triangular_solve | solution.py:104
  579.3 32.5 %copy-start.7 = (f32[128]{0:T(128)S(1)}, f32[128]{0:T(128)}, u32[]{:S(2)}) copy-start(f32[128]{0:T(128)} %copy-done.6) | copy-start | bytes 1540
  579.3 32.6 %copy-start.9 = (f32[128]{0:T(128)S(1)}, f32[128]{0:T(128)}, u32[]{:S(2)}) copy-start(f32[128]{0:T(128)} %copy-done.8) | copy-start | bytes 1540
  581.4 108.0 %copy-start.11 = (f32[16]{0:T(128)S(1)}, f32[16]{0:T(128)}, u32[]{:S(2)}) copy-start(f32[16]{0:T(128)} %copy-done.10) | copy-start | bytes 196
  581.4 5.5 collective-permute-start.5
  584.8 5.7 collective-permute-start.6
  590.5 21.3 %collective-permute-start.7 = (f32[16,10,1,128]{3,0,2,1:T(8,128)S(1)}, f32[16,10,1,128]{3,0,2,1:T(8,128)S(1)}, u32[]{:S(2)}, u32[]{:S(2)}) collective-permute-start(f32[16,10,1,128]{3,0,2,1:T(8,128)S(1)} %get-tuple-element.44), channel_id=1, source_target_pairs={{0,1},{1,2},{2,3},{3,4},{4,5},{5,6},{6,7},{8,9},{9,10},{10,11},{11... | collective-permute-start | bytes 245768 | tf_op jit(solution)/shard_map/ppermute | solution.py:19
  594.2 17.6 %collective-permute-start.8 = (f32[16,10,1,128]{3,0,2,1:T(8,128)S(1)}, f32[16,10,1,128]{3,0,2,1:T(8,128)S(1)}, u32[]{:S(2)}, u32[]{:S(2)}) collective-permute-start(f32[16,10,1,128]{3,0,2,1:T(8,128)S(1)} %get-tuple-element.45), channel_id=1, source_target_pairs={{1,0},{2,1},{3,2},{4,3},{5,4},{6,5},{7,6},{9,8},{10,9},{11,10},{12... | collective-permute-start | bytes 245768 | tf_op jit(solution)/shard_map/ppermute | solution.py:20
Sparse Core Ops, SparseCore 0:
  73.6 146.4 all-reduce.4
